TPU v7x, 32 devices: a whole 2x2x4 slice. The times are simulated.
32 devices in a mesh: groups: 2 (over y), tm: 4 (over z), space: 2 (over x), chan: 2 (over core).
Axes of the slice: x: 2, y: 2, z: 4, core: 2. Of those that a mesh axis runs over, the one named last changes fastest.
Arguments:
- activations: bfloat16 [256, 8, 16, 256], P(('groups', 'chan'), 'tm', 'space'), parts along dimension 0
- frame_clip: int32 [16], P(('groups', 'tm')), parts along dimension 0, may hold values from 0 to 3, as said below
- conv_weight: bfloat16 [3, 3, 3, 128, 128], replicated, may hold values from -0.109375 to 0.109375
- norm_gain: float32 [128], replicated, may hold values from 0.25 to 1.75
- norm_bias: float32 [128], replicated, may hold values from -3 to 3
- out_weight: bfloat16 [2, 2, 128, 32], replicated, may hold values from -0.25 to 0.25
- owner: int32 [4, 32, 1], P(('groups', 'space'), 'tm'), parts along dimension 0, may hold values from 0 to 3; in each aligned block of 8 rows (0 to 7, 8 to 15, ..., all dimensions but the last counted through in order) at most 4 rows name the same one
Outputs:
- owned: bfloat16 [4, 64, 32, 128], P(('groups', 'space'), 'tm', 'chan'), parts along dimension 0
There are 2 independent parts, one for each index of `groups`. A program takes and returns all parts, laid end to end along the dimension named above; an argument that names none is the same for every part. Nothing has to cross between parts.
Inputs may be any that keep to these rules, and one draw needn't show every extreme that they name: `frame_clip`: clip numbers never fall along the frames; each clip has 1 to 4 frames and one has exactly 4. Among the 8 rows of one tm index (aligned blocks), no owner is named more than 4 times; some owner is named exactly 4 times in some block.
All inputs are finite; a program needn't handle non-finite values.
Results may differ from a plain program's by a relative error of at most 0.012.
Values may be sent and summed in bfloat16 or wider, within the bound.
A program may use at most 64 MiB of HBM per device.

v0:
```python
import jax
import jax.numpy as jnp
from jax import lax
from jax.sharding import PartitionSpec as P

CHANNELS = 128
GROUPS = 32
CLIPS = 4
MOMENTS = 32


def shifted(value, axis, steps):
    count = lax.axis_size(axis)
    leading, last = (max(0, -steps), min(count, count - steps))
    return lax.ppermute(value, axis, [(source, source + steps) for source in range(leading, last)])


def with_halo(block, sides, width):
    for axis, dim in sides:
        count = lax.axis_size(axis)
        forward = [(i, i + 1) for i in range(count - 1)]
        backward = [(target, source) for source, target in forward]
        low = lax.ppermute(
            lax.slice_in_dim(block, block.shape[dim] - width, None, axis=dim), axis, forward
        )
        high = lax.ppermute(lax.slice_in_dim(block, 0, width, axis=dim), axis, backward)
        block = jnp.concatenate([low, block, high], axis=dim)
    return block


def plane_conv(frames, kernel):
    return lax.conv_general_dilated(
        frames,
        kernel,
        (1, 1),
        ((0, 0), (1, 1)),
        dimension_numbers=("CNHW", "HWIO", "CNHW"),
        preferred_element_type=jnp.float32,
    )


def shards(activations, frame_clip, conv_weight, norm_gain, norm_bias, out_weight, owner):
    c_local, frames_here, rows_here, columns = activations.shape
    chan_index = lax.axis_index("chan")
    chan_first = chan_index * c_local
    trailing_ids = (frame_clip + 1).astype(jnp.bfloat16)
    previous, previous_ids = shifted((activations, trailing_ids), "tm", 1)
    extended = jnp.concatenate([previous, activations], axis=1)
    extended_ids = jnp.concatenate(
        [previous_ids.astype(jnp.float32), (frame_clip + 1).astype(jnp.float32)]
    )
    padded = with_halo(extended, (("space", 2),), 1)
    own_ids = extended_ids[2:]
    matches = [(extended_ids[m : m + frames_here] == own_ids).astype(jnp.int32) for m in range(3)]
    position = jnp.arange(frames_here, dtype=jnp.int32)
    tap_index = []
    for k in range(3):
        number = matches[k]
        for m in range(k + 1, 3):
            number = number + matches[m]
        tap_index.append(position + 3 - number)
    chan_count = lax.axis_size("chan")
    window = frames_here // chan_count
    windows = jnp.stack(
        [padded[:, w * window : w * window + window + 2] for w in range(chan_count)], axis=1
    )
    whole_window = lax.all_to_all(windows, "chan", split_axis=1, concat_axis=0, tiled=True)[:, 0]
    window_start = chan_index * window
    running = None
    for k in range(3):
        local_taps = lax.dynamic_slice_in_dim(tap_index[k], window_start, window) - window_start
        term = plane_conv(jnp.take(whole_window, local_taps, axis=1), conv_weight[k])
        running = term if running is None else running + term
    conv_window = running.astype(jnp.bfloat16)
    conv_full = lax.all_to_all(conv_window, "chan", split_axis=0, concat_axis=1, tiled=True).astype(
        jnp.float32
    )
    conv_value = conv_full.astype(jnp.bfloat16).astype(jnp.float32)
    group_size = CHANNELS // GROUPS
    local_groups = c_local // group_size
    onehot = (frame_clip[:, None] == jnp.arange(CLIPS, dtype=jnp.int32)[None, :]).astype(
        jnp.float32
    )
    sums_one = (
        jnp.sum(conv_value, axis=(2, 3)).reshape(local_groups, group_size, frames_here).sum(1)
    )
    sums_two = (
        jnp.sum(conv_value * conv_value, axis=(2, 3))
        .reshape(local_groups, group_size, frames_here)
        .sum(1)
    )
    sums_one = jnp.dot(sums_one, onehot, precision=lax.Precision.HIGHEST)
    sums_two = jnp.dot(sums_two, onehot, precision=lax.Precision.HIGHEST)
    counts_here = jnp.sum(onehot, axis=0) * (rows_here * columns * group_size)
    sums_one, sums_two, counts = lax.psum((sums_one, sums_two, counts_here), ("tm", "space"))
    mean = sums_one / counts
    rstd = lax.rsqrt(sums_two / counts - mean * mean + 1e-06)
    mean_frame = jnp.repeat(
        jnp.dot(mean, onehot.T, precision=lax.Precision.HIGHEST), group_size, axis=0
    )
    rstd_frame = jnp.repeat(
        jnp.dot(rstd, onehot.T, precision=lax.Precision.HIGHEST), group_size, axis=0
    )
    gain_here = lax.dynamic_slice_in_dim(norm_gain, chan_first, c_local)
    bias_here = lax.dynamic_slice_in_dim(norm_bias, chan_first, c_local)
    scaled = (conv_value - mean_frame[:, :, None, None]) * rstd_frame[:, :, None, None]
    normed = jax.nn.silu(
        scaled * gain_here[:, None, None, None] + bias_here[:, None, None, None]
    ).astype(jnp.bfloat16)
    patches = normed.reshape(c_local, frames_here, rows_here // 2, 2, columns // 2, 2)
    weight_here = lax.dynamic_slice(out_weight, (0, 0, chan_first, 0), (2, 2, c_local, MOMENTS))
    latent = lax.psum_scatter(
        jnp.einsum("cfrizj,ijco->ofrz", patches, weight_here, preferred_element_type=jnp.float32),
        "chan",
        scatter_dimension=0,
        tiled=True,
    ).astype(jnp.bfloat16)
    moments_here = latent.shape[0]
    send_rows = frames_here * (rows_here // 2)
    row_block = latent.reshape(moments_here, send_rows, columns // 2)
    tm_size = lax.axis_size("tm")
    capacity = max(2, 2 * send_rows // tm_size)
    targets = owner[0, :, 0]
    earlier = jnp.arange(send_rows)[None, :] < jnp.arange(send_rows)[:, None]
    equal = targets[:, None] == targets[None, :]
    order_rank = jnp.sum((equal & earlier).astype(jnp.int32), axis=1)
    slot_of_row = targets * capacity + order_rank
    selector = (
        slot_of_row[None, :] == jnp.arange(tm_size * capacity, dtype=jnp.int32)[:, None]
    ).astype(jnp.bfloat16)
    outgoing = jnp.einsum(
        "sr,crw->scw", selector, row_block, preferred_element_type=jnp.float32
    ).astype(jnp.bfloat16)
    arrived = lax.all_to_all(outgoing, "tm", split_axis=0, concat_axis=0, tiled=True)
    return arrived[None]


def solution(mesh):
    placed = (
        P(("groups", "chan"), "tm", "space", None),
        P(("groups", "tm")),
        P(),
        P(),
        P(),
        P(),
        P(("groups", "space"), "tm", None),
    )
    return jax.shard_map(
        shards,
        mesh=mesh,
        in_specs=placed,
        out_specs=P(("groups", "space"), "tm", "chan", None),
        check_vma=False,
    )
```

profile of v0, /device:TPU:0, one launch (start us, length us, event | category | flops | bytes accessed | tf_op | source)
XLA Modules:
  0.0 105.7 jit_solution(17287263570309921566)
XLA Ops:
  6.5 1.3 %copy.97 = bf16[64,2,8,256]{3,0,2,1:T(8,128)(2,1)S(1)} copy(bf16[64,2,8,256]{3,2,1,0:T(8,128)(2,1)} %param.9) | data formatting | bytes 1048576 | tf_op args[0]
  7.8 5.0 %collective-permute-start = (bf16[64,2,8,256]{3,0,2,1:T(8,128)(2,1)S(1)}, bf16[64,2,8,256]{3,0,2,1:T(8,128)(2,1)S(1)}, u32[]{:S(2)}, u32[]{:S(2)}) collective-permute-start(bf16[64,2,8,256]{3,0,2,1:T(8,128)(2,1)S(1)} %copy.97), channel_id=1, source_target_pairs={{0,4},{4,8},{8,12},{1,5},{5,9},{9,13},{2,6},{6,10},{10,14},{3,7},{... | collective-permute-start | bytes 1572872 | tf_op jit(solution)/shard_map/ppermute | solution.py:15
  12.8 0.7 add_convert_fusion.1
  13.5 3.4 %collective-permute-start.3 = (bf16[2]{0:T(256)(128)(2,1)S(1)}, bf16[2]{0:T(256)(128)(2,1)S(1)}, u32[]{:S(2)}, u32[]{:S(2)}) collective-permute-start(bf16[2]{0:T(256)(128)(2,1)S(1)} %get-tuple-element.32), channel_id=1, source_target_pairs={{0,4},{4,8},{8,12},{1,5},{5,9},{9,13},{2,6},{6,10},{10,14},{3,7},{... | collective-permute-start | bytes 20 | tf_op jit(solution)/shard_map/ppermute | solution.py:15
  16.9 0.7 dynamic_slice.23
  17.7 0.7 dynamic_slice.22
  18.4 0.7 convert_reduce_fusion.1
  19.1 4.9 %collective-permute-done.3 = bf16[2]{0:T(256)(128)(2,1)S(1)} collective-permute-done((bf16[2]{0:T(256)(128)(2,1)S(1)}, bf16[2]{0:T(256)(128)(2,1)S(1)}, u32[]{:S(2)}, u32[]{:S(2)}) %collective-permute-start.3) | collective-permute-done | bytes 36 | tf_op jit(solution)/shard_map/ppermute | solution.py:15
  24.0 0.1 pad_maximum_fusion.2
  24.1 0.2 constant_dynamic-update-slice_fusion
  24.3 1.3 %collective-permute-start.2 = (bf16[64,4,1,256]{3,0,2,1:T(8,128)(2,1)S(1)}, bf16[64,4,1,256]{3,0,2,1:T(8,128)(2,1)S(1)}, u32[]{:S(2)}, u32[]{:S(2)}) collective-permute-start(bf16[64,4,1,256]{3,0,2,1:T(8,128)(2,1)S(1)} %get-tuple-element.28), channel_id=1, source_target_pairs={{2,0},{3,1},{6,4},{7,5},{10,8},{11,9},{14,12},{15,13},{18,16},{19,... | collective-permute-start | bytes 393224 | tf_op jit(solution)/shard_map/ppermute | solution.py:26
  25.6 4.6 %collective-permute-start.1 = (bf16[64,4,1,256]{3,0,2,1:T(8,128)(2,1)S(1)}, bf16[64,4,1,256]{3,0,2,1:T(8,128)(2,1)S(1)}, u32[]{:S(2)}, u32[]{:S(2)}) collective-permute-start(bf16[64,4,1,256]{3,0,2,1:T(8,128)(2,1)S(1)} %get-tuple-element.27), channel_id=1, source_target_pairs={{0,2},{1,3},{4,6},{5,7},{8,10},{9,11},{12,14},{13,15},{16,18},{17,... | collective-permute-start | bytes 393224 | tf_op jit(solution)/shard_map/ppermute | solution.py:23
  30.2 0.1 fusion.52
  30.3 0.7 dynamic_slice.21
  31.6 0.7 dynamic_slice.20
  33.0 0.6 dynamic_slice.19
  34.3 0.2 pad_maximum_fusion.1
  34.5 0.2 slice_bitcast_fusion.1
  34.7 0.2 pad_maximum_fusion
  34.9 5.3 %all_to_all.29 = bf16[64,2,3,10,256]{4,0,3,2,1:T(8,128)(2,1)S(1)} all-to-all(bf16[64,2,3,10,256]{4,0,3,2,1:T(8,128)(2,1)S(1)} %pad_maximum_fusion), channel_id=1, replica_groups=mesh['groups'=2,'tm'=4,'space'=2,'chan'=2] {'chan'}, dimensions={1} | all-to-all | bytes 3932160 | tf_op jit(solution)/shard_map/all_to_all | solution.py:67
  40.2 0.2 copy.99
  40.5 0.2 select_bitcast_fusion
  40.6 0.4 copy.119
  41.0 0.2 pad.4.clone
  41.2 0.2 reshape.82
  41.4 0.1 copy.105
  41.6 0.3 copy.118
  41.9 0.2 pad.2.clone
  42.1 0.2 reshape.77
  42.3 0.1 copy.102
  42.4 0.8 copy-done.2
  43.3 0.3 copy.120
  43.6 0.2 pad.6.clone
  43.8 0.2 reshape.87
  44.0 0.1 copy.108
  44.2 0.3 copy-done.7
  44.5 0.7 copy-done.5
  45.2 1.5 %convolution_select_fusion.1 = f32[8,8,33,128]{3,1,2,0:T(8,128)S(1)} fusion(bf16[128,10,1,7,2]{0,3,4,1,2:T(8,128)(2,1)S(1)} %slice.52, bf16[128,10,1,8,33]{0,3,4,1,2:T(8,128)(2,1)S(1)} %copy.105, pred[8,33]{0,1:T(8,128)(4,1)S(1)} %copy-done.7, bf16[3,3,3,128,128]{4,3,2,1,0:T(8,128)(2,1)S(1)} %copy-done.5), kind=kOutput, calls=%fused_computation.6 | convolution fusion | flops 625274880 | bytes 2098176 | tf_op jit(solution)/shard_map/conv_general_dilated | solution.py:32
  46.7 1.5 %fusion.3 = f32[8,8,33,128]{3,1,2,0:T(8,128)S(1)} fusion(f32[8,8,33,128]{3,1,2,0:T(8,128)S(1)} %convolution_select_fusion.1, bf16[128,10,1,7,2]{0,3,4,1,2:T(8,128)(2,1)S(1)} %slice.51, bf16[128,10,1,8,33]{0,3,4,1,2:T(8,128)(2,1)S(1)} %copy-done.3, pred[8,33]{0,1:T(8,128)(4,1)S(1)} %copy-done.7, bf16[3,3,3,128,128]{4,3,2,1,0:T(8,128)(2,1)S(1)} %copy-done.5), kind=kOutput, calls=%fused_computation.8 | convolution fusion | flops 625545216 | bytes 3179520 | tf_op jit(solution)/shard_map/conv_general_dilated | solution.py:32
  48.2 1.5 %fusion.5 = bf16[8,8,33,128]{3,1,2,0:T(8,128)(2,1)S(1)} fusion(f32[8,8,33,128]{3,1,2,0:T(8,128)S(1)} %fusion.3, bf16[128,10,1,7,2]{0,3,4,1,2:T(8,128)(2,1)S(1)} %slice.53, bf16[128,10,1,8,33]{0,3,4,1,2:T(8,128)(2,1)S(1)} %copy.108, pred[8,33]{0,1:T(8,128)(4,1)S(1)} %copy-done.7, bf16[3,3,3,128,128]{4,3,2,1,0:T(8,128)(2,1)S(1)} %copy-done.5), kind=kOutput, calls=%fused_computation.11 | convolution fusion | flops 625815552 | bytes 2638848 | tf_op jit(solution)/shard_map/conv_general_dilated | solution.py:32
  49.8 0.6 copy.110
  50.3 4.2 %all_to_all.30 = bf16[128,1,8,256]{3,2,1,0:T(8,128)(2,1)S(1)} all-to-all(bf16[128,1,8,256]{3,2,1,0:T(8,128)(2,1)S(1)} %copy.110), channel_id=1, replica_groups=mesh['groups'=2,'tm'=4,'space'=2,'chan'=2] {'chan'}, dimensions={0} | all-to-all | bytes 1048576 | tf_op jit(solution)/shard_map/all_to_all | solution.py:75
  54.5 0.1 convert_bitcast_fusion
  54.6 0.6 fusion.24
  55.1 0.6 copy.112
  55.8 0.9 copy.113
  56.7 0.1 reshape.48
  56.8 0.1 reduce_sum.59
  56.9 0.3 fusion.46
  57.1 0.1 reshape.47
  57.2 0.1 reduce_sum.56
  57.3 0.3 fusion.48
  57.6 22.1 %all-reduce = (f32[16,4]{0,1:T(4,128)S(1)}, f32[4]{0:T(128)S(1)}, f32[16,4]{0,1:T(4,128)S(1)}) all-reduce(f32[16,4]{0,1:T(4,128)S(1)} %fusion.46, f32[4]{0:T(128)S(1)} %broadcast_multiply_fusion, f32[16,4]{0,1:T(4,128)S(1)} %fusion.48), channel_id=1, replica_groups=mesh['groups'=2,'tm'=4,'space'=2,'chan'=2] {'tm','space'}, use_global_device_ids=true, to_apply=%region_8.10 | all-reduce | flops 132 | bytes 1056 | tf_op jit(solution)/shard_map/psum | solution.py:95
  79.7 0.2 fusion.47
  79.9 0.2 fusion.40
  80.2 0.1 mul.50
  80.4 0.1 sub.44
  80.5 1.2 %convolution_bitcast_fusion = f32[32,2,4,128]{3,0,2,1:T(8,128)} fusion(f32[64,2,4,2,128,2]{4,0,5,3,2,1:T(8,128)S(1)} %copy.113, f32[64]{0:T(128)S(1)} %dynamic_slice.23, f32[64]{0:T(128)S(1)} %dynamic_slice.22, f32[64,2]{0,1:T(2,128)S(1)} %mul.50, f32[64,2]{0,1:T(2,128)S(1)} %sub.44, bf16[2,2,128,32]{2,3,1,0:T(8,128)(2,1)S(1)} %copy-done, s32[]{:T(128)S(6)} %select_n.25), kind=kOutput, calls=%fused_computation.12 | convolution fusion | flops 19136512 | bytes 1213956 | tf_op jit(solution)/shard_map/cfrizj,ijco->ofrz/dot_general | solution.py:113
  81.7 0.2 convert_reduce_fusion
  81.9 4.8 %reduce-scatter.2.cloned.1.call-done = f32[16,2,4,128]{3,0,2,1:T(8,128)} async-done(((f32[32,2,4,128]{3,0,2,1:T(8,128)}), f32[16,2,4,128]{3,0,2,1:T(8,128)}) %reduce-scatter.2.cloned.1.call-update) | async-done | bytes 65552 | tf_op jit(solution)/shard_map/reduce_scatter | solution.py:112
  86.7 0.8 convert_element_type.73
  87.6 0.3 convolution_convert_fusion
  87.9 10.3 %all_to_all.31 = bf16[16,16,128]{2,1,0:T(8,128)(2,1)S(1)} all-to-all(bf16[16,16,128]{2,1,0:T(8,128)(2,1)S(1)} %copy.115), channel_id=1, replica_groups=mesh['groups'=2,'tm'=4,'space'=2,'chan'=2] {'tm'}, dimensions={0} | all-to-all | bytes 131072 | tf_op jit(solution)/shard_map/all_to_all | solution.py:134
  98.2 0.6 copy.126
  (31 shorter events, 0.4 us)
Async XLA Ops:
  6.5 73.9 %copy-start = (bf16[2,2,128,32]{2,3,1,0:T(8,128)(2,1)S(1)}, bf16[2,2,128,32]{2,3,1,0:T(8,128)(2,1)}, u32[]{:S(2)}) copy-start(bf16[2,2,128,32]{2,3,1,0:T(8,128)(2,1)} %param.14) | copy-start | bytes 98308
  6.5 17.6 %copy-start.1 = (bf16[64,2,8,256]{3,2,1,0:T(8,128)(2,1)S(1)}, bf16[64,2,8,256]{3,2,1,0:T(8,128)(2,1)}, u32[]{:S(2)}) copy-start(bf16[64,2,8,256]{3,2,1,0:T(8,128)(2,1)} %param.9) | copy-start | bytes 1572868
  6.5 80.2 %reduce-scatter.2.cloned.1.call-start = ((), (), s32[]{:S(2)}) async-start(), calls=%async_computation.4 | async-start | bytes 196608 | tf_op jit(solution)/shard_map/reduce_scatter | solution.py:112
  7.8 22.4 %copy-start.4 = (s32[2]{0:T(128)S(1)}, s32[2]{0:T(128)}, u32[]{:S(2)}) copy-start(s32[2]{0:T(128)} %param.10) | copy-start | bytes 28
  7.8 16.3 %collective-permute-start = (bf16[64,2,8,256]{3,0,2,1:T(8,128)(2,1)S(1)}, bf16[64,2,8,256]{3,0,2,1:T(8,128)(2,1)S(1)}, u32[]{:S(2)}, u32[]{:S(2)}) collective-permute-start(bf16[64,2,8,256]{3,0,2,1:T(8,128)(2,1)S(1)} %copy.97), channel_id=1, source_target_pairs={{0,4},{4,8},{8,12},{1,5},{5,9},{9,13},{2,6},{6,10},{10,14},{3,7},{... | collective-permute-start | bytes 1572872 | tf_op jit(solution)/shard_map/ppermute | solution.py:15
  13.5 10.5 %collective-permute-start.3 = (bf16[2]{0:T(256)(128)(2,1)S(1)}, bf16[2]{0:T(256)(128)(2,1)S(1)}, u32[]{:S(2)}, u32[]{:S(2)}) collective-permute-start(bf16[2]{0:T(256)(128)(2,1)S(1)} %get-tuple-element.32), channel_id=1, source_target_pairs={{0,4},{4,8},{8,12},{1,5},{5,9},{9,13},{2,6},{6,10},{10,14},{3,7},{... | collective-permute-start | bytes 20 | tf_op jit(solution)/shard_map/ppermute | solution.py:15
  24.3 10.0 %collective-permute-start.2 = (bf16[64,4,1,256]{3,0,2,1:T(8,128)(2,1)S(1)}, bf16[64,4,1,256]{3,0,2,1:T(8,128)(2,1)S(1)}, u32[]{:S(2)}, u32[]{:S(2)}) collective-permute-start(bf16[64,4,1,256]{3,0,2,1:T(8,128)(2,1)S(1)} %get-tuple-element.28), channel_id=1, source_target_pairs={{2,0},{3,1},{6,4},{7,5},{10,8},{11,9},{14,12},{15,13},{18,16},{19,... | collective-permute-start | bytes 393224 | tf_op jit(solution)/shard_map/ppermute | solution.py:26
  25.6 8.7 %collective-permute-start.1 = (bf16[64,4,1,256]{3,0,2,1:T(8,128)(2,1)S(1)}, bf16[64,4,1,256]{3,0,2,1:T(8,128)(2,1)S(1)}, u32[]{:S(2)}, u32[]{:S(2)}) collective-permute-start(bf16[64,4,1,256]{3,0,2,1:T(8,128)(2,1)S(1)} %get-tuple-element.27), channel_id=1, source_target_pairs={{0,2},{1,3},{4,6},{5,7},{8,10},{9,11},{12,14},{13,15},{16,18},{17,... | collective-permute-start | bytes 393224 | tf_op jit(solution)/shard_map/ppermute | solution.py:23
  42.4 0.9 copy-start.2
  43.8 0.7 copy-start.7
  44.0 1.2 %copy-start.5 = (bf16[3,3,3,128,128]{4,3,2,1,0:T(8,128)(2,1)S(1)}, bf16[3,3,3,128,128]{4,3,2,1,0:T(8,128)(2,1)}, u32[]{:S(2)}) copy-start(bf16[3,3,3,128,128]{4,3,2,1,0:T(8,128)(2,1)} %param.11) | copy-start | bytes 2654212
  45.2 1.5 %copy-start.3 = (bf16[128,10,1,8,33]{0,3,4,1,2:T(8,128)(2,1)S(1)}, bf16[128,10,1,8,33]{0,3,4,1,2:T(8,128)(2,1)}, u32[]{:S(2)}) copy-start(bf16[128,10,1,8,33]{0,3,4,1,2:T(8,128)(2,1)} %copy-done.2) | copy-start | bytes 2027524
  80.5 1.2 %copy-start.6 = (s32[1,8,1]{1,2,0:T(1,128)S(1)}, s32[1,8,1]{1,2,0:T(1,128)}, u32[]{:S(2)}) copy-start(s32[1,8,1]{1,2,0:T(1,128)} %param.15) | copy-start | bytes 100
Sparse Core Ops, SparseCore 0:
  81.8 4.8 reduce-scatter.1
where the time goes:
time: 106 us
  blocking collectives  42 us (40%)
  between operations  15.9 us (15%)
  starting transfers between devices  14.3 us (13%)
  local copies, waits for them, and re-layouts  13.1 us (12%)
  waiting for transfers between devices  9.71 us (9%)
  matrix products  6.8 us (6%)
  other arithmetic  3.95 us (4%)
    psum x1, blocking collectives, shards(): lax.psum((sums_one, sums_two, counts_here), ('tm', 'space'))  22.1 us
    all_to_all x1, blocking collectives, shards(): lax.all_to_all(outgoing, 'tm', split_axis=0, concat_axis=0, tiled=True)  10.3 us
    ppermute x2, starting transfers between devices, shifted(): lax.ppermute(value, axis, [(source, source + steps) for source in range(l...  8.43 us
    all_to_all x1, blocking collectives, shards(): lax.all_to_all(windows, 'chan', split_axis=1, concat_axis=0, tiled=True)  5.31 us
    unnamed x22, local copies, waits for them, and re-layouts  4.86 us
    ppermute x2, waiting for transfers between devices, shifted(): lax.ppermute(value, axis, [(source, source + steps) for source in range(l...  4.86 us
    reduce_scatter x1, waiting for transfers between devices, shards(): lax.psum_scatter(jnp.einsum('cfrizj,ijco->ofrz', patches, weight_here, pr...  4.83 us
    ppermute x1, starting transfers between devices, with_halo(): lax.ppermute(lax.slice_in_dim(block, block.shape[dim] - width, None, axis...  4.56 us
  transfers between devices with their start and end apart: 5, of which 2 were waited for; matrix products, arithmetic and copies ran while one was open for 5% of the time, Pallas kernels for 0%

commit v1 on v0

v1 whole, which is shorter than its diff:
```python
import functools

import jax
import jax.numpy as jnp
from jax import lax
from jax.experimental import pallas as pl
from jax.experimental.pallas import tpu as pltpu
from jax.sharding import PartitionSpec as P

CHANNELS = 128
GROUPS = 32
GROUP_SIZE = CHANNELS // GROUPS
F32 = jnp.float32
BF16 = jnp.bfloat16
MESH = pl.DeviceIdType.MESH


def kernel(
    sizes, act, meta_in, weight, gain, bias, out_weight, out,
    x, wt, conv, stat, stats, latent, arrived, meta, ids, sums,
    near_send, near_recv, zrow_send, zrow_recv, meta_send, meta_recv, stat_send, stat_recv,
    lat_send, lat_recv, extra_send, extra_recv, local_sem,
):
    n_tm, n_space, capacity, chunks = sizes
    frames_here, rows, half, columns = act.shape
    lanes = columns // 2
    total = n_tm * n_space * 2
    n_frames = n_tm * frames_here
    lat_rows = rows // 2
    step_rows = rows // chunks
    t = lax.axis_index("tm")
    s = lax.axis_index("space")
    c = lax.axis_index("chan")
    me = (t * n_space + s) * 2 + c
    first = jnp.logical_and(t == 0, c == 1)
    has_main = jnp.logical_or(c == 1, t < n_tm - 1)

    def where_is(flat):
        return {"tm": flat // (2 * n_space), "space": (flat // 2) % n_space, "chan": flat % 2}

    barrier = pltpu.get_barrier_semaphore()

    @pl.loop(1, total)
    def _(step):
        pl.semaphore_signal(
            barrier, inc=1, device_id=where_is(lax.rem(me + step, total)), device_id_type=MESH
        )

    pl.semaphore_wait(barrier, total - 1)

    def remote(src, dst, send, recv, device):
        return pltpu.make_async_remote_copy(
            src_ref=src, dst_ref=dst, send_sem=send, recv_sem=recv, device_id=device,
            device_id_type=MESH,
        )

    def meta_copy(target):
        return remote(
            meta_in, meta.at[t], meta_send.at[target], meta_recv.at[t],
            {"tm": target, "space": s, "chan": c},
        )

    @pl.loop(1, n_tm)
    def _(step):
        meta_copy(lax.rem(t + step, n_tm)).start()

    up_ok, down_ok = t < n_tm - 1, t > 0
    t_up, t_down = jnp.minimum(t + 1, n_tm - 1), jnp.maximum(t - 1, 0)

    def zrow(up, piece):
        frame, slot, core, tt = (1, 0, 1, t_up) if up else (0, 2, 0, t_down)
        return remote(
            act.at[frame, pl.ds(piece * step_rows, step_rows)],
            x.at[slot, pl.ds(1 + piece * step_rows, step_rows), c],
            zrow_send.at[int(up), piece], zrow_recv.at[c, piece],
            {"tm": tt, "space": s, "chan": core},
        )

    def space_of(low):
        return jnp.maximum(s - 1, 0) if low else jnp.minimum(s + 1, n_space - 1)

    def edge(low, core):
        return remote(
            act.at[:, 0 if low else rows - 1],
            x.at[pl.ds(core, 2), rows + 1 if low else 0, c],
            near_send.at[int(low) * 2 + core], near_recv.at[int(low) * 2 + c],
            {"tm": t, "space": space_of(low), "chan": core},
        )

    def zedge(up, low):
        frame, slot, core, tt = (1, 0, 1, t_up) if up else (0, 2, 0, t_down)
        return remote(
            act.at[frame, 0 if low else rows - 1],
            x.at[slot, rows + 1 if low else 0, c],
            near_send.at[4 + int(low) * 2 + int(up)], near_recv.at[4 + int(low) * 2 + c],
            {"tm": tt, "space": space_of(low), "chan": core},
        )

    peer = remote(
        act, x.at[pl.ds(1 - c, 2), pl.ds(1, rows), c], near_send.at[8], near_recv.at[8],
        {"tm": t, "space": s, "chan": 1 - c},
    )
    low_ok, high_ok = s > 0, s < n_space - 1
    sides = ((True, low_ok), (False, high_ok))
    zs = ((True, up_ok), (False, down_ok))

    peer.start()
    for low, ok in sides:
        for up, z_ok in zs:
            @pl.when(jnp.logical_and(ok, z_ok))
            def _(low=low, up=up):
                zedge(up, low).start()
    for piece in range(chunks):
        for up, z_ok in zs:
            @pl.when(z_ok)
            def _(piece=piece, up=up):
                zrow(up, piece).start()
    for low, ok in sides:
        @pl.when(ok)
        def _(low=low):
            edge(low, 0).start()
            edge(low, 1).start()

    meta[t] = meta_in[...]
    for f in range(2):
        x[c + f, pl.ds(1, rows), c] = act[f]
    zero_row = jnp.zeros((3, 2, half, columns), BF16)

    @pl.when(s == 0)
    def _():
        x[:, 0] = zero_row

    @pl.when(s == n_space - 1)
    def _():
        x[:, rows + 1] = zero_row

    @pl.when(first)
    def _():
        x[0, pl.ds(1, rows)] = jnp.zeros((rows, 2, half, columns), BF16)

        @pl.when(s > 0)
        def _():
            x[0, 0] = zero_row[0]

        @pl.when(s < n_space - 1)
        def _():
            x[0, rows + 1] = zero_row[0]

    for k in range(3):
        for i in range(3):
            for j in range(3):
                wt[k, pl.ds(j * 128, 128), pl.ds(i * 128, 128)] = weight[k, i, j].T
    stat[...] = jnp.zeros_like(stat)

    @pl.loop(1, n_tm)
    def _(step):
        source = lax.rem(t + step, n_tm)
        remote(
            meta_in, meta.at[source], meta_send.at[source], meta_recv.at[source],
            {"tm": source, "space": s, "chan": c},
        ).wait_recv()

    to_scalars = pltpu.make_async_copy(meta, ids, local_sem)
    to_scalars.start()
    to_scalars.wait()

    def clip_of(frame):
        frame = jnp.minimum(frame, n_frames - 1)
        return ids[frame // 2, 0, frame % 2]

    my_frame = 2 * t + 2 - c
    my_clip = clip_of(my_frame)
    older = jnp.logical_and(my_frame >= 2, clip_of(jnp.maximum(my_frame - 2, 0)) == my_clip)
    newer = clip_of(jnp.maximum(my_frame - 1, 0)) == my_clip

    peer.wait_recv()
    for low, ok in ((True, high_ok), (False, low_ok)):
        for core in range(2):
            @pl.when(ok)
            def _(low=low, core=core):
                remote(
                    act.at[:, 0], x.at[pl.ds(c, 2), rows + 1 if low else 0, core],
                    near_send.at[int(low) * 2 + core], near_recv.at[int(low) * 2 + core],
                    {"tm": t, "space": s, "chan": c},
                ).wait_recv()

    lane = lax.broadcasted_iota(jnp.int32, (CHANNELS, columns), 1)

    def conv_row(h, kept, taps):
        acc = None
        for k in range(3):
            term = jnp.dot(wt[k], taps[k](h), preferred_element_type=F32)
            acc = term if acc is None else acc + term
        left = jnp.where(lane == 0, 0.0, pltpu.roll(acc[0:128], 1, 1))
        right = jnp.where(lane == columns - 1, 0.0, pltpu.roll(acc[256:384], columns - 1, 1))
        value = (left + acc[128:256] + right).astype(BF16)
        conv[kept, h] = value
        value = value.astype(F32)
        a, b = value[:, :lanes], value[:, lanes:]
        sums[0] += a + b
        sums[1] += a * a + b * b

    def slab(slot):
        return lambda h: x[slot, pl.ds(h, 3)].reshape(3 * CHANNELS, columns)

    def sums_to(row):
        stat[pl.ds(row, 1), :] = jnp.sum(sums[0].T, axis=0, keepdims=True)
        stat[pl.ds(row + 1, 1), :] = jnp.sum(sums[1].T, axis=0, keepdims=True)

    @pl.when(first)
    def _():
        sums[...] = jnp.zeros_like(sums)

        @pl.loop(0, rows)
        def _(h):
            conv_row(h, 1, [slab(1)] * 3)

        sums_to(2)

    gets_z = jnp.logical_or(jnp.logical_and(c == 1, down_ok), jnp.logical_and(c == 0, up_ok))
    z_slot = 2 * (1 - c)

    def wait_zedge(low, ok):
        for core in range(2):
            @pl.when(jnp.logical_and(gets_z, ok))
            def _(core=core):
                remote(
                    act.at[0, 0], x.at[z_slot, rows + 1 if low else 0, core],
                    near_send.at[4 + int(low) * 2], near_recv.at[4 + int(low) * 2 + core],
                    {"tm": t, "space": s, "chan": c},
                ).wait_recv()

    def wait_zrow(piece):
        for core in range(2):
            @pl.when(gets_z)
            def _(core=core):
                remote(
                    act.at[0, pl.ds(piece * step_rows, step_rows)],
                    x.at[z_slot, pl.ds(1 + piece * step_rows, step_rows), core],
                    zrow_send.at[0, piece], zrow_recv.at[core, piece],
                    {"tm": t, "space": s, "chan": c},
                ).wait_recv()

    def tap_old(h):
        return jnp.where(older, slab(0)(h), tap_mid(h))

    def tap_mid(h):
        return jnp.where(newer, slab(1)(h), slab(2)(h))

    taps = [tap_old, tap_mid, slab(2)]
    wait_zedge(False, low_ok)
    wait_zedge(True, high_ok)

    @pl.when(has_main)
    def _():
        sums[...] = jnp.zeros_like(sums)

    for piece in range(chunks):
        wait_zrow(piece)
        begin = 0 if piece == 0 else piece * step_rows - 1
        end = rows if piece == chunks - 1 else (piece + 1) * step_rows - 1

        @pl.when(has_main)
        def _(begin=begin, end=end):
            @pl.loop(begin, end)
            def _(h):
                conv_row(h, 0, taps)

    @pl.when(has_main)
    def _():
        sums_to(0)

    def stat_copy(target):
        return remote(
            stat, stats.at[me], stat_send.at[target], stat_recv.at[me], where_is(target)
        )

    stats[me] = stat[...]

    @pl.loop(1, total)
    def _(step):
        stat_copy(lax.rem(me + step, total)).start()

    gain_c = jnp.broadcast_to(gain[...], (128, 128)).T
    bias_c = jnp.broadcast_to(bias[...], (128, 128)).T
    spread_row = lax.broadcasted_iota(jnp.int32, (columns, columns), 0)
    spread_col = lax.broadcasted_iota(jnp.int32, (columns, columns), 1)
    picked = jnp.where(spread_col < lanes, 2 * spread_col, 2 * (spread_col - lanes) + 1)
    spread = jnp.where(spread_row == picked, 1.0, 0.0).astype(BF16)

    @pl.loop(1, total)
    def _(step):
        source = lax.rem(me + step, total)
        remote(
            stat, stats.at[source], stat_send.at[source], stat_recv.at[source], where_is(source)
        ).wait_recv()

    lane8 = lax.broadcasted_iota(jnp.int32, (8, 128), 1)

    def group_sum(v):
        v = v + jnp.where(lane8 % 2 == 0, pltpu.roll(v, 127, 1), pltpu.roll(v, 1, 1))
        return v + jnp.where(lane8 % 4 < 2, pltpu.roll(v, 126, 1), pltpu.roll(v, 2, 1))

    def finish(kept, clip):
        def add_main(source, carry):
            frame = 2 * (source // (2 * n_space)) + 2 - source % 2
            same = jnp.logical_and(frame < n_frames, clip_of(frame) == clip)
            return carry + jnp.where(same, stats[source], 0.0)

        gathered = lax.fori_loop(0, total, add_main, jnp.zeros((8, 128), F32))
        zero_frame = jnp.zeros((8, 128), F32)
        for space in range(n_space):
            zero_frame += stats[2 * space + 1]
        zero_frame = jnp.where(clip_of(0) == clip, zero_frame, 0.0)
        number = jnp.float32(0)
        for frame in range(n_frames):
            number += jnp.where(clip_of(frame) == clip, 1.0, 0.0)
        count = number * float(rows * n_space * columns * GROUP_SIZE)
        gathered = group_sum(gathered)
        zero_frame = group_sum(zero_frame)
        count = jnp.broadcast_to(count, (1, 128))
        mean = (gathered[0:1] + zero_frame[2:3]) / count
        var = (gathered[1:2] + zero_frame[3:4]) / count - mean * mean
        rstd = lax.rsqrt(var + 1e-6)
        mean_c = jnp.broadcast_to(mean, (128, 128)).T
        scale_c = jnp.broadcast_to(rstd, (128, 128)).T * gain_c

        @pl.loop(0, lat_rows)
        def _(r):
            parts = []
            for i in range(2):
                value = conv[kept, 2 * r + i].astype(F32)
                pieces = []
                for u in range(2):
                    v = (value[:, u * lanes:(u + 1) * lanes] - mean_c) * scale_c + bias_c
                    pieces.append((v / (1.0 + jnp.exp(-v))).astype(BF16))
                normed = jnp.concatenate(pieces, axis=1)
                sorted_ = jnp.dot(normed, spread, preferred_element_type=F32).astype(BF16)
                parts += [sorted_[:, :lanes], sorted_[:, lanes:]]
            stacked = jnp.concatenate(parts, axis=0)
            result = lax.dot_general(
                out_weight[...], stacked, (((0,), (0,)), ((), ())), preferred_element_type=F32
            ).astype(BF16)
            latent[kept, 0, r] = result[0:16]
            latent[kept, 1, r] = result[16:32]

    def lat_copy(kept, frame, target, core, send, recv):
        return remote(
            latent.at[kept, core], arrived.at[frame], send.at[target * 2 + core], recv,
            {"tm": target, "space": s, "chan": core},
        )

    here = t * 2 + c
    places = n_tm * 2

    def send_latent(kept, frame, send, recv):
        arrived[frame] = latent[kept, c]

        @pl.loop(1, places)
        def _(step):
            target = lax.rem(here + step, places)
            lat_copy(kept, frame, target // 2, target % 2, send, recv).start()

    @pl.when(first)
    def _():
        finish(1, clip_of(0))
        send_latent(1, 0, extra_send, extra_recv)

    @pl.when(has_main)
    def _():
        finish(0, my_clip)
        send_latent(0, my_frame, lat_send, lat_recv.at[my_frame])

    @pl.loop(1, n_frames)
    def _(frame):
        @pl.when(frame != my_frame)
        def _():
            lat_copy(0, frame, t, c, lat_send, lat_recv.at[frame]).wait_recv()

    @pl.when(jnp.logical_not(first))
    def _():
        lat_copy(0, 0, t, c, lat_send, extra_recv).wait_recv()

    @pl.loop(0, n_tm)
    def _(b):
        taken = jnp.int32(0)
        slots = []
        for n in range(2 * lat_rows):
            hit = ids[b, 0, frames_here + n] == t
            slots.append(jnp.where(hit, taken, -1))
            taken = taken + jnp.where(hit, 1, 0)
        for j in range(capacity):
            value = jnp.zeros((16, lanes), BF16)
            for n in range(2 * lat_rows):
                row = arrived[2 * b + n // lat_rows, n % lat_rows]
                value = jnp.where(slots[n] == j, row, value)
            out[0, b * capacity + j] = value

    @pl.loop(1, n_tm)
    def _(step):
        meta_copy(lax.rem(t + step, n_tm)).wait_send()

    peer.wait_send()
    for low, ok in sides:
        for up, z_ok in zs:
            @pl.when(jnp.logical_and(ok, z_ok))
            def _(low=low, up=up):
                zedge(up, low).wait_send()

        @pl.when(ok)
        def _(low=low):
            edge(low, 0).wait_send()
            edge(low, 1).wait_send()
    for piece in range(chunks):
        for up, z_ok in zs:
            @pl.when(z_ok)
            def _(piece=piece, up=up):
                zrow(up, piece).wait_send()

    @pl.loop(1, total)
    def _(step):
        stat_copy(lax.rem(me + step, total)).wait_send()

    def latents_left(kept, frame, send, recv):
        @pl.loop(1, places)
        def _(step):
            target = lax.rem(here + step, places)
            lat_copy(kept, frame, target // 2, target % 2, send, recv).wait_send()

    @pl.when(first)
    def _():
        latents_left(1, 0, extra_send, extra_recv)

    @pl.when(has_main)
    def _():
        latents_left(0, my_frame, lat_send, lat_recv.at[my_frame])


def solution(mesh):
    n_tm, n_space = mesh.shape["tm"], mesh.shape["space"]
    total = n_tm * n_space * 2

    def shards(activations, frame_clip, conv_weight, norm_gain, norm_bias, out_weight, owner):
        half, frames_here, rows, columns = activations.shape
        lat_rows = rows // 2
        capacity = max(2, 2 * frames_here * lat_rows // n_tm)
        chunks = 4
        act = activations.transpose(1, 2, 0, 3)
        numbers = jnp.concatenate([frame_clip, owner.reshape(-1)])
        meta = jnp.zeros((8, 128), jnp.int32).at[0, : numbers.shape[0]].set(numbers)
        moments = out_weight.shape[-1]
        dma = pltpu.SemaphoreType.DMA
        return pl.pallas_call(
            functools.partial(kernel, (n_tm, n_space, capacity, chunks)),
            out_shape=jax.ShapeDtypeStruct(
                (1, n_tm * capacity, moments // 2, columns // 2), BF16
            ),
            in_specs=[pl.BlockSpec(memory_space=pltpu.VMEM)] * 6,
            out_specs=pl.BlockSpec(memory_space=pltpu.VMEM),
            scratch_shapes=[
                pltpu.VMEM((3, rows + 2, 2, half, columns), BF16),
                pltpu.VMEM((3, 384, 384), BF16),
                pltpu.VMEM((2, rows, CHANNELS, columns), BF16),
                pltpu.VMEM((8, 128), F32),
                pltpu.VMEM((total, 8, 128), F32),
                pltpu.VMEM((2, 2, lat_rows, moments // 2, columns // 2), BF16),
                pltpu.VMEM((n_tm * frames_here, lat_rows, moments // 2, columns // 2), BF16),
                pltpu.VMEM((n_tm, 8, 128), jnp.int32),
                pltpu.SMEM((n_tm, 8, 128), jnp.int32),
                pltpu.VMEM((2, CHANNELS, columns // 2), F32),
                dma((9,)),
                dma((9,)),
                dma((2, chunks)),
                dma((2, chunks)),
                dma((n_tm,)),
                dma((n_tm,)),
                dma((total,)),
                dma((total,)),
                dma((2 * n_tm,)),
                dma((n_tm * frames_here,)),
                dma((2 * n_tm,)),
                dma(()),
                dma(()),
            ],
            compiler_params=pltpu.CompilerParams(
                collective_id=0, has_side_effects=True, vmem_limit_bytes=48 << 20
            ),
        )(
            act, meta, conv_weight, norm_gain.reshape(1, -1), norm_bias.reshape(1, -1),
            out_weight.reshape(-1, moments),
        )

    placed = (
        P(("groups", "chan"), "tm", "space", None),
        P(("groups", "tm")),
        P(),
        P(),
        P(),
        P(),
        P(("groups", "space"), "tm", None),
    )
    return jax.shard_map(
        shards,
        mesh=mesh,
        in_specs=placed,
        out_specs=P(("groups", "space"), "tm", "chan", None),
        check_vma=False,
    )
```

time: 106 us -> 35.6 us (0.34)
  blocking collectives: 42 us -> 0 us
  Pallas kernels: 0 us -> 31.1 us
  between operations: 15.9 us -> 0.04 us
  starting transfers between devices: 14.3 us -> 0 us
  local copies, waits for them, and re-layouts: 13.1 us -> 3.37 us
  waiting for transfers between devices: 9.71 us -> 0 us
  matrix products: 6.8 us -> 0 us
  other arithmetic: 3.95 us -> 0.83 us
    pallas_call x0 -> x1, Pallas kernels: none -> 31.1 us  [shards(): pl.pallas_call(functools.partial(kernel, (n_tm, n_space, capacity, chunks...]
    psum x1 -> x0, blocking collectives: 22.1 us -> none  [shards(): lax.psum((sums_one, sums_two, counts_here), ('tm', 'space'))]
    all_to_all x3 -> x0, blocking collectives: 19.8 us -> none  [the longest x1 10.3 us: shards(): lax.all_to_all(outgoing, 'tm', split_axis=0, concat_axis=0, tiled=True)]
    ppermute x4 -> x0, starting transfers between devices: 14.3 us -> none  [the longest x2 8.43 us: shifted(): lax.ppermute(value, axis, [(source, source + steps) for source in range(l...]
    ppermute x4 -> x0, waiting for transfers between devices: 4.86 us -> none  [the longest x2 4.86 us: shifted(): lax.ppermute(value, axis, [(source, source + steps) for source in range(l...]
    reduce_scatter x1 -> x0, waiting for transfers between devices: 4.83 us -> none  [shards(): lax.psum_scatter(jnp.einsum('cfrizj,ijco->ofrz', patches, weight_here, pr...]
    conv_general_dilated x3 -> x0, matrix products: 4.42 us -> none  [plane_conv(): lax.conv_general_dilated(frames, kernel, (1, 1), ((0, 0), (1, 1)), dimens...]
    dynamic_slice x5 -> x0, local copies, waits for them, and re-layouts: 3.41 us -> none  [the longest x3 1.95 us: shards(): lax.dynamic_slice_in_dim(tap_index[k], window_start, window) - window_start]
  transfers between devices with their start and end apart: 5 -> 0, of which waited for: 2 -> 0; matrix products, arithmetic and copies ran while one was open for 5% -> 0% of each run, Pallas kernels for 0% -> 0%
where the time goes in v1:
time: 35.6 us; the launch traced here: 35.3 us
  Pallas kernels  31.1 us (87%)
  local copies, waits for them, and re-layouts  3.37 us (9%)
  other arithmetic  0.83 us (2%)
    pallas_call x1, Pallas kernels, shards(): pl.pallas_call(functools.partial(kernel, (n_tm, n_space, capacity, chunks...  31.1 us
    unnamed x9, local copies, waits for them, and re-layouts  3.36 us
    another operation x1, other arithmetic  0.83 us

profile of v1, /device:TPU:0, one launch (start us, length us, event | category | flops | bytes accessed | tf_op | source)
XLA Modules:
  0.0 35.3 jit_solution(17973628985530362770)
XLA Ops:
  0.0 0.0 copy-start
  0.0 0.8 %add_bitcast_fusion = s32[1,10]{1,0:T(1,128)S(1)} fusion(s32[8]{0:T(128)} %bitcast.13, s32[2]{0:T(128)} %param.10), kind=kLoop, calls=%fused_computation.1 | loop fusion | flops 10 | bytes 80 | tf_op jit(solution)/shard_map/reshape.31
  0.8 0.9 %copy.9 = bf16[2,2,128,32]{3,2,1,0:T(8,128)(2,1)S(1)} copy(bf16[2,2,128,32]{2,3,1,0:T(8,128)(2,1)} %param.14) | data formatting | bytes 65536 | tf_op args[5]
  1.7 1.2 %copy.11 = bf16[64,2,8,256]{3,0,2,1:T(8,128)(2,1)S(1)} copy(bf16[64,2,8,256]{3,2,1,0:T(8,128)(2,1)} %param.9) | data formatting | bytes 1048576 | tf_op args[0]
  2.9 0.0 copy-start.1
  2.9 0.0 copy-start.2
  2.9 0.0 copy-done
  3.0 0.6 %copy-done.1 = f32[128]{0:T(128)S(1)} copy-done((f32[128]{0:T(128)S(1)}, f32[128]{0:T(128)}, u32[]{:S(2)}) %copy-start.1) | copy-done | bytes 536
  3.6 0.0 copy-done.2
  3.6 31.1 %shard_map.73 = bf16[1,16,16,128]{3,2,1,0:T(8,128)(2,1)S(1)} custom-call(bf16[2,8,64,256]{3,2,1,0:T(8,128)(2,1)S(1)} %bitcast.9, s32[8,128]{1,0:T(8,128)S(1)} %scatter.4.meta_in, bf16[3,3,3,128,128]{4,3,2,1,0:T(8,128)(2,1)S(1)} %copy-done, f32[1,128]{1,0:T(1,128)S(1)} %bitcast.11, f32[1,128]{1,0:T(1,128)S(1)} %bitcast.12, bf16[512,32]{1,0:T(8,128)(2,1)S(1)} %bitcast.10), custom_call_target="tpu_custom_call" | custom-call | tf_op jit(solution)/shard_map/pallas_call | solution.py:453
  34.7 0.6 %copy.13 = bf16[1,16,16,128]{3,2,1,0:T(8,128)(2,1)} copy(bf16[1,16,16,128]{3,2,1,0:T(8,128)(2,1)S(1)} %shard_map.73) | data formatting | bytes 131072
  (1 shorter events, 0.0 us)
Async XLA Ops:
  0.0 2.9 %copy-start = (bf16[3,3,3,128,128]{4,3,2,1,0:T(8,128)(2,1)S(1)}, bf16[3,3,3,128,128]{4,3,2,1,0:T(8,128)(2,1)}, u32[]{:S(2)}) copy-start(bf16[3,3,3,128,128]{4,3,2,1,0:T(8,128)(2,1)} %weight.1) | copy-start | bytes 2654212
  2.9 0.7 %copy-start.1 = (f32[128]{0:T(128)S(1)}, f32[128]{0:T(128)}, u32[]{:S(2)}) copy-start(f32[128]{0:T(128)} %param.12) | copy-start | bytes 1540
  2.9 0.7 %copy-start.2 = (f32[128]{0:T(128)S(1)}, f32[128]{0:T(128)}, u32[]{:S(2)}) copy-start(f32[128]{0:T(128)} %param.13) | copy-start | bytes 1540

commit v2 on v1

--- a/solution.py
+++ b/solution.py
@@ -16,7 +16,8 @@
 
 
 def kernel(
-    sizes, act, meta_in, weight, gain, bias, out_weight, out,
+    sizes, clip_hbm, owner_hbm, act_in, weight_in, gain_in, bias_in, out_weight_in, out,
+    clip_in, owner_in, act_raw, act, weight, gain, bias, out_weight, meta_in,
     x, wt, conv, stat, stats, latent, arrived, meta, ids, sums,
     near_send, near_recv, zrow_send, zrow_recv, meta_send, meta_recv, stat_send, stat_recv,
     lat_send, lat_recv, extra_send, extra_recv, local_sem,
@@ -32,12 +33,27 @@
     s = lax.axis_index("space")
     c = lax.axis_index("chan")
     me = (t * n_space + s) * 2 + c
-    first = jnp.logical_and(t == 0, c == 1)
+    first = t == 0
+    piece_rows = lat_rows // 2
+    reach = n_tm // 2
     has_main = jnp.logical_or(c == 1, t < n_tm - 1)
 
     def where_is(flat):
         return {"tm": flat // (2 * n_space), "space": (flat // 2) % n_space, "chan": flat % 2}
 
+    fetches = [
+        pltpu.make_async_copy(source, held, local_sem.at[1 + n])
+        for n, (source, held) in enumerate((
+            (act_in, act_raw), (weight_in, weight), (gain_in, gain), (bias_in, bias),
+            (out_weight_in, out_weight),
+            (clip_hbm, clip_in), (owner_hbm, owner_in),
+        ))
+    ]
+    for fetch in fetches:
+        fetch.start()
+    stats[...] = jnp.zeros_like(stats)
+    stat[...] = jnp.zeros_like(stat)
+
     barrier = pltpu.get_barrier_semaphore()
 
     @pl.loop(1, total)
@@ -45,6 +61,22 @@
         pl.semaphore_signal(
             barrier, inc=1, device_id=where_is(lax.rem(me + step, total)), device_id_type=MESH
         )
+
+    fetches[5].wait()
+    fetches[6].wait()
+    place = lax.broadcasted_iota(jnp.int32, (8, 128), 1)
+    numbers = jnp.zeros((8, 128), jnp.int32)
+    for n in range(frames_here):
+        numbers = jnp.where(place == n, clip_in[0, n], numbers)
+    for n in range(frames_here * lat_rows):
+        numbers = jnp.where(place == frames_here + n, owner_in[0, n], numbers)
+    meta_in[...] = numbers
+    meta[t] = numbers
+    fetches[0].wait()
+    for f in range(frames_here):
+        turned = jnp.transpose(act_raw[:, f], (1, 0, 2))
+        act[f] = turned
+        x[c + f, pl.ds(1, rows), c] = turned
 
     pl.semaphore_wait(barrier, total - 1)
 
@@ -121,9 +153,6 @@
             edge(low, 0).start()
             edge(low, 1).start()
 
-    meta[t] = meta_in[...]
-    for f in range(2):
-        x[c + f, pl.ds(1, rows), c] = act[f]
     zero_row = jnp.zeros((3, 2, half, columns), BF16)
 
     @pl.when(s == 0)
@@ -134,7 +163,7 @@
     def _():
         x[:, rows + 1] = zero_row
 
-    @pl.when(first)
+    @pl.when(jnp.logical_and(first, c == 1))
     def _():
         x[0, pl.ds(1, rows)] = jnp.zeros((rows, 2, half, columns), BF16)
 
@@ -146,11 +175,14 @@
         def _():
             x[0, rows + 1] = zero_row[0]
 
+    for fetch in fetches[1:5]:
+        fetch.wait()
     for k in range(3):
         for i in range(3):
             for j in range(3):
                 wt[k, pl.ds(j * 128, 128), pl.ds(i * 128, 128)] = weight[k, i, j].T
-    stat[...] = jnp.zeros_like(stat)
+    gain_c = jnp.broadcast_to(gain[...], (128, 128)).T
+    bias_c = jnp.broadcast_to(bias[...], (128, 128)).T * 0.5
 
     @pl.loop(1, n_tm)
     def _(step):
@@ -160,7 +192,7 @@
             {"tm": source, "space": s, "chan": c},
         ).wait_recv()
 
-    to_scalars = pltpu.make_async_copy(meta, ids, local_sem)
+    to_scalars = pltpu.make_async_copy(meta, ids, local_sem.at[0])
     to_scalars.start()
     to_scalars.wait()
 
@@ -211,9 +243,9 @@
     def _():
         sums[...] = jnp.zeros_like(sums)
 
-        @pl.loop(0, rows)
+        @pl.loop(c * (rows // 2), (c + 1) * (rows // 2))
         def _(h):
-            conv_row(h, 1, [slab(1)] * 3)
+            conv_row(h, 1, [slab(c)] * 3)
 
         sums_to(2)
 
@@ -277,12 +309,17 @@
 
     stats[me] = stat[...]
 
+    def near(device):
+        return jnp.abs(device // (2 * n_space) - t) <= reach
+
     @pl.loop(1, total)
     def _(step):
-        stat_copy(lax.rem(me + step, total)).start()
-
-    gain_c = jnp.broadcast_to(gain[...], (128, 128)).T
-    bias_c = jnp.broadcast_to(bias[...], (128, 128)).T
+        target = lax.rem(me + step, total)
+
+        @pl.when(near(target))
+        def _():
+            stat_copy(target).start()
+
     spread_row = lax.broadcasted_iota(jnp.int32, (columns, columns), 0)
     spread_col = lax.broadcasted_iota(jnp.int32, (columns, columns), 1)
     picked = jnp.where(spread_col < lanes, 2 * spread_col, 2 * (spread_col - lanes) + 1)
@@ -291,9 +328,13 @@
     @pl.loop(1, total)
     def _(step):
         source = lax.rem(me + step, total)
-        remote(
-            stat, stats.at[source], stat_send.at[source], stat_recv.at[source], where_is(source)
-        ).wait_recv()
+
+        @pl.when(near(source))
+        def _():
+            remote(
+                stat, stats.at[source], stat_send.at[source], stat_recv.at[source],
+                where_is(source),
+            ).wait_recv()
 
     lane8 = lax.broadcasted_iota(jnp.int32, (8, 128), 1)
 
@@ -301,7 +342,9 @@
         v = v + jnp.where(lane8 % 2 == 0, pltpu.roll(v, 127, 1), pltpu.roll(v, 1, 1))
         return v + jnp.where(lane8 % 4 < 2, pltpu.roll(v, 126, 1), pltpu.roll(v, 2, 1))
 
-    def finish(kept, clip):
+    weights = jnp.concatenate([out_weight[q] for q in range(4)], axis=1)
+
+    def moments_of(clip):
         def add_main(source, carry):
             frame = 2 * (source // (2 * n_space)) + 2 - source % 2
             same = jnp.logical_and(frame < n_frames, clip_of(frame) == clip)
@@ -309,8 +352,8 @@
 
         gathered = lax.fori_loop(0, total, add_main, jnp.zeros((8, 128), F32))
         zero_frame = jnp.zeros((8, 128), F32)
-        for space in range(n_space):
-            zero_frame += stats[2 * space + 1]
+        for n in range(2 * n_space):
+            zero_frame += stats[n]
         zero_frame = jnp.where(clip_of(0) == clip, zero_frame, 0.0)
         number = jnp.float32(0)
         for frame in range(n_frames):
@@ -323,63 +366,83 @@
         var = (gathered[1:2] + zero_frame[3:4]) / count - mean * mean
         rstd = lax.rsqrt(var + 1e-6)
         mean_c = jnp.broadcast_to(mean, (128, 128)).T
-        scale_c = jnp.broadcast_to(rstd, (128, 128)).T * gain_c
-
-        @pl.loop(0, lat_rows)
-        def _(r):
-            parts = []
-            for i in range(2):
-                value = conv[kept, 2 * r + i].astype(F32)
-                pieces = []
-                for u in range(2):
-                    v = (value[:, u * lanes:(u + 1) * lanes] - mean_c) * scale_c + bias_c
-                    pieces.append((v / (1.0 + jnp.exp(-v))).astype(BF16))
-                normed = jnp.concatenate(pieces, axis=1)
-                sorted_ = jnp.dot(normed, spread, preferred_element_type=F32).astype(BF16)
-                parts += [sorted_[:, :lanes], sorted_[:, lanes:]]
-            stacked = jnp.concatenate(parts, axis=0)
-            result = lax.dot_general(
-                out_weight[...], stacked, (((0,), (0,)), ((), ())), preferred_element_type=F32
-            ).astype(BF16)
-            latent[kept, 0, r] = result[0:16]
-            latent[kept, 1, r] = result[16:32]
-
-    def lat_copy(kept, frame, target, core, send, recv):
+        scale_c = jnp.broadcast_to(rstd, (128, 128)).T * gain_c * 0.5
+        return mean_c, scale_c
+
+    def finish(kept, piece, mean_c, scale_c):
+        rows_in = []
+        for q in range(2 * piece_rows):
+            value = conv[kept, 2 * piece_rows * piece + q].astype(F32)
+            pieces = []
+            for u in range(2):
+                v = (value[:, u * lanes:(u + 1) * lanes] - mean_c) * scale_c + bias_c
+                pieces.append((v + v * jnp.tanh(v)).astype(BF16))
+            rows_in.append(jnp.concatenate(pieces, axis=1))
+        sorted_ = jnp.dot(
+            jnp.concatenate(rows_in, axis=0), spread, preferred_element_type=F32
+        ).astype(BF16)
+        wide = jnp.concatenate(
+            [
+                jnp.concatenate(
+                    [
+                        sorted_[(2 * r + i) * 128:(2 * r + i + 1) * 128, j * lanes:(j + 1) * lanes]
+                        for i in range(2) for j in range(2)
+                    ],
+                    axis=0,
+                )
+                for r in range(piece_rows)
+            ],
+            axis=1,
+        )
+        result = jnp.dot(weights, wide, preferred_element_type=F32).astype(BF16)
+        for r in range(piece_rows):
+            latent[kept, 0, piece * piece_rows + r] = result[0:16, r * lanes:(r + 1) * lanes]
+            latent[kept, 1, piece * piece_rows + r] = result[16:32, r * lanes:(r + 1) * lanes]
+
+    def lat_copy(kept, piece, frame, target, core, send, recv):
+        span = pl.ds(piece * piece_rows, piece_rows)
         return remote(
-            latent.at[kept, core], arrived.at[frame], send.at[target * 2 + core], recv,
+            latent.at[kept, core, span], arrived.at[frame, span], send.at[target * 2 + core], recv,
             {"tm": target, "space": s, "chan": core},
         )
 
     here = t * 2 + c
     places = n_tm * 2
 
-    def send_latent(kept, frame, send, recv):
-        arrived[frame] = latent[kept, c]
+    def send_latent(kept, piece, frame, send, recv):
+        span = pl.ds(piece * piece_rows, piece_rows)
+        arrived[frame, span] = latent[kept, c, span]
 
         @pl.loop(1, places)
         def _(step):
             target = lax.rem(here + step, places)
-            lat_copy(kept, frame, target // 2, target % 2, send, recv).start()
+            lat_copy(kept, piece, frame, target // 2, target % 2, send, recv).start()
 
     @pl.when(first)
     def _():
-        finish(1, clip_of(0))
-        send_latent(1, 0, extra_send, extra_recv)
+        finish(1, c, *moments_of(clip_of(0)))
+        send_latent(1, c, 0, extra_send, extra_recv.at[c])
 
     @pl.when(has_main)
     def _():
-        finish(0, my_clip)
-        send_latent(0, my_frame, lat_send, lat_recv.at[my_frame])
+        found = moments_of(my_clip)
+        for piece in range(2):
+            finish(0, piece, *found)
+            send_latent(0, piece, my_frame, lat_send.at[piece], lat_recv.at[my_frame, piece])
 
     @pl.loop(1, n_frames)
     def _(frame):
         @pl.when(frame != my_frame)
         def _():
-            lat_copy(0, frame, t, c, lat_send, lat_recv.at[frame]).wait_recv()
-
-    @pl.when(jnp.logical_not(first))
-    def _():
-        lat_copy(0, 0, t, c, lat_send, extra_recv).wait_recv()
+            for piece in range(2):
+                lat_copy(
+                    0, piece, frame, t, c, lat_send.at[piece], lat_recv.at[frame, piece]
+                ).wait_recv()
+
+    for piece in range(2):
+        @pl.when(jnp.logical_not(jnp.logical_and(first, c == piece)))
+        def _(piece=piece):
+            lat_copy(0, piece, 0, t, c, lat_send.at[piece], extra_recv.at[piece]).wait_recv()
 
     @pl.loop(0, n_tm)
     def _(b):
@@ -419,21 +482,26 @@
 
     @pl.loop(1, total)
     def _(step):
-        stat_copy(lax.rem(me + step, total)).wait_send()
-
-    def latents_left(kept, frame, send, recv):
+        target = lax.rem(me + step, total)
+
+        @pl.when(near(target))
+        def _():
+            stat_copy(target).wait_send()
+
+    def latents_left(kept, piece, frame, send, recv):
         @pl.loop(1, places)
         def _(step):
             target = lax.rem(here + step, places)
-            lat_copy(kept, frame, target // 2, target % 2, send, recv).wait_send()
+            lat_copy(kept, piece, frame, target // 2, target % 2, send, recv).wait_send()
 
     @pl.when(first)
     def _():
-        latents_left(1, 0, extra_send, extra_recv)
+        latents_left(1, c, 0, extra_send, extra_recv.at[c])
 
     @pl.when(has_main)
     def _():
-        latents_left(0, my_frame, lat_send, lat_recv.at[my_frame])
+        for piece in range(2):
+            latents_left(0, piece, my_frame, lat_send.at[piece], lat_recv.at[my_frame, piece])
 
 
 def solution(mesh):
@@ -444,10 +512,7 @@
         half, frames_here, rows, columns = activations.shape
         lat_rows = rows // 2
         capacity = max(2, 2 * frames_here * lat_rows // n_tm)
-        chunks = 4
-        act = activations.transpose(1, 2, 0, 3)
-        numbers = jnp.concatenate([frame_clip, owner.reshape(-1)])
-        meta = jnp.zeros((8, 128), jnp.int32).at[0, : numbers.shape[0]].set(numbers)
+        chunks = rows
         moments = out_weight.shape[-1]
         dma = pltpu.SemaphoreType.DMA
         return pl.pallas_call(
@@ -455,9 +520,18 @@
             out_shape=jax.ShapeDtypeStruct(
                 (1, n_tm * capacity, moments // 2, columns // 2), BF16
             ),
-            in_specs=[pl.BlockSpec(memory_space=pltpu.VMEM)] * 6,
+            in_specs=[pl.BlockSpec(memory_space=pltpu.HBM)] * 7,
             out_specs=pl.BlockSpec(memory_space=pltpu.VMEM),
             scratch_shapes=[
+                pltpu.SMEM((1, frames_here), jnp.int32),
+                pltpu.SMEM((1, frames_here * lat_rows), jnp.int32),
+                pltpu.VMEM(activations.shape, BF16),
+                pltpu.VMEM((frames_here, rows, half, columns), BF16),
+                pltpu.VMEM(conv_weight.shape, BF16),
+                pltpu.VMEM((1, CHANNELS), F32),
+                pltpu.VMEM((1, CHANNELS), F32),
+                pltpu.VMEM((4, moments, CHANNELS), BF16),
+                pltpu.VMEM((8, 128), jnp.int32),
                 pltpu.VMEM((3, rows + 2, 2, half, columns), BF16),
                 pltpu.VMEM((3, 384, 384), BF16),
                 pltpu.VMEM((2, rows, CHANNELS, columns), BF16),
@@ -476,18 +550,19 @@
                 dma((n_tm,)),
                 dma((total,)),
                 dma((total,)),
+                dma((2, 2 * n_tm)),
+                dma((n_tm * frames_here, 2)),
                 dma((2 * n_tm,)),
-                dma((n_tm * frames_here,)),
-                dma((2 * n_tm,)),
-                dma(()),
-                dma(()),
+                dma((2,)),
+                dma((8,)),
             ],
             compiler_params=pltpu.CompilerParams(
-                collective_id=0, has_side_effects=True, vmem_limit_bytes=48 << 20
+                collective_id=0, has_side_effects=True, vmem_limit_bytes=67_043_328
             ),
         )(
-            act, meta, conv_weight, norm_gain.reshape(1, -1), norm_bias.reshape(1, -1),
-            out_weight.reshape(-1, moments),
+            frame_clip.reshape(1, -1), owner.reshape(1, -1), activations, conv_weight,
+            norm_gain.reshape(1, -1), norm_bias.reshape(1, -1),
+            out_weight.transpose(0, 1, 3, 2).reshape(4, moments, CHANNELS),
         )
 
     placed = (

time: 35.6 us -> 30.8 us (0.87)
  Pallas kernels: 31.1 us -> 29.2 us
  local copies, waits for them, and re-layouts: 3.37 us -> 1.47 us
  other arithmetic: 0.83 us -> 0 us
    pallas_call x1, Pallas kernels: 31.1 us -> 29.2 us  [shards(): pl.pallas_call(functools.partial(kernel, (n_tm, n_space, capacity, chunks...]
    unnamed x9 -> x1, local copies, waits for them, and re-layouts: 3.36 us -> 1.47 us
    another operation x1 -> x0, other arithmetic: 0.83 us -> none
where the time goes in v2:
time: 30.8 us; the launch traced here: 30.7 us
  Pallas kernels  29.2 us (95%)
  local copies, waits for them, and re-layouts  1.47 us (5%)
    pallas_call x1, Pallas kernels, shards(): pl.pallas_call(functools.partial(kernel, (n_tm, n_space, capacity, chunks...  29.2 us
    unnamed x1, local copies, waits for them, and re-layouts  1.47 us

profile of v2, /device:TPU:0, one launch (start us, length us, event | category | flops | bytes accessed | tf_op | source)
XLA Modules:
  0.0 30.7 jit_solution(8501523618342789290)
XLA Ops:
  0.0 29.2 %shard_map.73 = bf16[1,16,16,128]{3,2,1,0:T(8,128)(2,1)} custom-call(s32[1,2]{1,0:T(1,128)} %bitcast.8, s32[1,8]{1,0:T(1,128)} %bitcast.9, bf16[64,2,8,256]{3,2,1,0:T(8,128)(2,1)} %act_in.1, bf16[3,3,3,128,128]{4,3,2,1,0:T(8,128)(2,1)} %weight_in.1, f32[1,128]{1,0:T(1,128)} %bitcast.10, f32[1,128]{1,0:T(1,128)} %bitcast.11, bf16[4,32,128]{2,1,0:T(8,128)(2,1)} %bitcast.7), custom_call_target="tpu_custom_call" | custom-call | tf_op jit(solution)/shard_map/pallas_call | solution.py:518
  29.2 1.5 %copy.9 = bf16[1,16,16,128]{3,2,1,0:T(8,128)(2,1)} copy(bf16[1,16,16,128]{3,2,1,0:T(8,128)(2,1)} %shard_map.73) | data formatting | bytes 131072

commit v3 on v2

--- a/solution.py
+++ b/solution.py
@@ -18,7 +18,7 @@
 def kernel(
     sizes, clip_hbm, owner_hbm, act_in, weight_in, gain_in, bias_in, out_weight_in, out,
     clip_in, owner_in, act_raw, act, weight, gain, bias, out_weight, meta_in,
-    x, wt, conv, stat, stats, latent, arrived, meta, ids, sums,
+    x, wt, conv, stat, stats, latent, arrived, meta, ids, ids_near, sums,
     near_send, near_recv, zrow_send, zrow_recv, meta_send, meta_recv, stat_send, stat_recv,
     lat_send, lat_recv, extra_send, extra_recv, local_sem,
 ):
@@ -184,27 +184,6 @@
     gain_c = jnp.broadcast_to(gain[...], (128, 128)).T
     bias_c = jnp.broadcast_to(bias[...], (128, 128)).T * 0.5
 
-    @pl.loop(1, n_tm)
-    def _(step):
-        source = lax.rem(t + step, n_tm)
-        remote(
-            meta_in, meta.at[source], meta_send.at[source], meta_recv.at[source],
-            {"tm": source, "space": s, "chan": c},
-        ).wait_recv()
-
-    to_scalars = pltpu.make_async_copy(meta, ids, local_sem.at[0])
-    to_scalars.start()
-    to_scalars.wait()
-
-    def clip_of(frame):
-        frame = jnp.minimum(frame, n_frames - 1)
-        return ids[frame // 2, 0, frame % 2]
-
-    my_frame = 2 * t + 2 - c
-    my_clip = clip_of(my_frame)
-    older = jnp.logical_and(my_frame >= 2, clip_of(jnp.maximum(my_frame - 2, 0)) == my_clip)
-    newer = clip_of(jnp.maximum(my_frame - 1, 0)) == my_clip
-
     peer.wait_recv()
     for low, ok in ((True, high_ok), (False, low_ok)):
         for core in range(2):
@@ -250,6 +229,24 @@
         sums_to(2)
 
     gets_z = jnp.logical_or(jnp.logical_and(c == 1, down_ok), jnp.logical_and(c == 0, up_ok))
+    my_frame = 2 * t + 2 - c
+    t_near = jnp.where(gets_z, jnp.where(c == 1, t_down, t_up), t)
+
+    @pl.when(gets_z)
+    def _():
+        remote(
+            meta_in, meta.at[t_near], meta_send.at[t_near], meta_recv.at[t_near],
+            {"tm": t_near, "space": s, "chan": c},
+        ).wait_recv()
+
+    near_ids = pltpu.make_async_copy(meta.at[t_near], ids_near, local_sem.at[8])
+    near_ids.start()
+    near_ids.wait()
+    my_clip = jnp.where(c == 1, clip_in[0, 1], ids_near[0, 0])
+    newer = jnp.where(c == 1, clip_in[0, 0], clip_in[0, 1]) == my_clip
+    oldest = jnp.where(c == 1, ids_near[0, 1], clip_in[0, 0])
+    older = jnp.logical_and(my_frame >= 2, oldest == my_clip)
+
     z_slot = 2 * (1 - c)
 
     def wait_zedge(low, ok):
@@ -324,6 +321,40 @@
     spread_col = lax.broadcasted_iota(jnp.int32, (columns, columns), 1)
     picked = jnp.where(spread_col < lanes, 2 * spread_col, 2 * (spread_col - lanes) + 1)
     spread = jnp.where(spread_row == picked, 1.0, 0.0).astype(BF16)
+
+    def part_columns(kept, begin, end):
+        @pl.loop(begin, end)
+        def _(h):
+            conv[kept, h] = jnp.dot(
+                conv[kept, h], spread, preferred_element_type=F32
+            ).astype(BF16)
+
+    @pl.when(has_main)
+    def _():
+        part_columns(0, 0, rows)
+
+    @pl.when(first)
+    def _():
+        part_columns(1, c * (rows // 2), (c + 1) * (rows // 2))
+
+    @pl.loop(1, n_tm)
+    def _(step):
+        source = lax.rem(t + step, n_tm)
+
+        @pl.when(source != t_near)
+        def _():
+            remote(
+                meta_in, meta.at[source], meta_send.at[source], meta_recv.at[source],
+                {"tm": source, "space": s, "chan": c},
+            ).wait_recv()
+
+    to_scalars = pltpu.make_async_copy(meta, ids, local_sem.at[0])
+    to_scalars.start()
+    to_scalars.wait()
+
+    def clip_of(frame):
+        frame = jnp.minimum(frame, n_frames - 1)
+        return ids[frame // 2, 0, frame % 2]
 
     @pl.loop(1, total)
     def _(step):
@@ -370,30 +401,16 @@
         return mean_c, scale_c
 
     def finish(kept, piece, mean_c, scale_c):
-        rows_in = []
-        for q in range(2 * piece_rows):
-            value = conv[kept, 2 * piece_rows * piece + q].astype(F32)
-            pieces = []
-            for u in range(2):
-                v = (value[:, u * lanes:(u + 1) * lanes] - mean_c) * scale_c + bias_c
-                pieces.append((v + v * jnp.tanh(v)).astype(BF16))
-            rows_in.append(jnp.concatenate(pieces, axis=1))
-        sorted_ = jnp.dot(
-            jnp.concatenate(rows_in, axis=0), spread, preferred_element_type=F32
-        ).astype(BF16)
-        wide = jnp.concatenate(
-            [
-                jnp.concatenate(
-                    [
-                        sorted_[(2 * r + i) * 128:(2 * r + i + 1) * 128, j * lanes:(j + 1) * lanes]
-                        for i in range(2) for j in range(2)
-                    ],
-                    axis=0,
-                )
-                for r in range(piece_rows)
-            ],
-            axis=1,
-        )
+        wide = []
+        for r in range(piece_rows):
+            parts = []
+            for i in range(2):
+                value = conv[kept, 2 * piece_rows * piece + 2 * r + i].astype(F32)
+                for j in range(2):
+                    v = (value[:, j * lanes:(j + 1) * lanes] - mean_c) * scale_c + bias_c
+                    parts.append((v + v * jnp.tanh(v)).astype(BF16))
+            wide.append(jnp.concatenate(parts, axis=0))
+        wide = jnp.concatenate(wide, axis=1)
         result = jnp.dot(weights, wide, preferred_element_type=F32).astype(BF16)
         for r in range(piece_rows):
             latent[kept, 0, piece * piece_rows + r] = result[0:16, r * lanes:(r + 1) * lanes]
@@ -541,6 +558,7 @@
                 pltpu.VMEM((n_tm * frames_here, lat_rows, moments // 2, columns // 2), BF16),
                 pltpu.VMEM((n_tm, 8, 128), jnp.int32),
                 pltpu.SMEM((n_tm, 8, 128), jnp.int32),
+                pltpu.SMEM((8, 128), jnp.int32),
                 pltpu.VMEM((2, CHANNELS, columns // 2), F32),
                 dma((9,)),
                 dma((9,)),
@@ -554,7 +572,7 @@
                 dma((n_tm * frames_here, 2)),
                 dma((2 * n_tm,)),
                 dma((2,)),
-                dma((8,)),
+                dma((9,)),
             ],
             compiler_params=pltpu.CompilerParams(
                 collective_id=0, has_side_effects=True, vmem_limit_bytes=67_043_328

time: 30.8 us -> 31.1 us (level)
    pallas_call x1, Pallas kernels: 29.2 us -> 29.5 us  [shards(): pl.pallas_call(functools.partial(kernel, (n_tm, n_space, capacity, chunks...]
where the time goes in v3:
time: 31.1 us; the launch traced here: 31 us
  Pallas kernels  29.5 us (95%)
  local copies, waits for them, and re-layouts  1.47 us (5%)
    pallas_call x1, Pallas kernels, shards(): pl.pallas_call(functools.partial(kernel, (n_tm, n_space, capacity, chunks...  29.5 us
    unnamed x1, local copies, waits for them, and re-layouts  1.47 us

profile of v3, /device:TPU:0, one launch (start us, length us, event | category | flops | bytes accessed | tf_op | source)
XLA Modules:
  0.0 31.0 jit_solution(14338381531942726092)
XLA Ops:
  0.0 29.5 %shard_map.73 = bf16[1,16,16,128]{3,2,1,0:T(8,128)(2,1)} custom-call(s32[1,2]{1,0:T(1,128)} %bitcast.8, s32[1,8]{1,0:T(1,128)} %bitcast.9, bf16[64,2,8,256]{3,2,1,0:T(8,128)(2,1)} %act_in.1, bf16[3,3,3,128,128]{4,3,2,1,0:T(8,128)(2,1)} %weight_in.1, f32[1,128]{1,0:T(1,128)} %bitcast.10, f32[1,128]{1,0:T(1,128)} %bitcast.11, bf16[4,32,128]{2,1,0:T(8,128)(2,1)} %bitcast.7), custom_call_target="tpu_custom_call" | custom-call | tf_op jit(solution)/shard_map/pallas_call | solution.py:535
  29.5 1.5 %copy.9 = bf16[1,16,16,128]{3,2,1,0:T(8,128)(2,1)} copy(bf16[1,16,16,128]{3,2,1,0:T(8,128)(2,1)} %shard_map.73) | data formatting | bytes 131072

commit v4 on v3

--- a/solution.py
+++ b/solution.py
@@ -136,7 +136,6 @@
     sides = ((True, low_ok), (False, high_ok))
     zs = ((True, up_ok), (False, down_ok))
 
-    peer.start()
     for low, ok in sides:
         for up, z_ok in zs:
             @pl.when(jnp.logical_and(ok, z_ok))
@@ -152,6 +151,8 @@
         def _(low=low):
             edge(low, 0).start()
             edge(low, 1).start()
+
+    peer.start()
 
     zero_row = jnp.zeros((3, 2, half, columns), BF16)
 
@@ -529,7 +530,7 @@
         half, frames_here, rows, columns = activations.shape
         lat_rows = rows // 2
         capacity = max(2, 2 * frames_here * lat_rows // n_tm)
-        chunks = rows
+        chunks = 2
         moments = out_weight.shape[-1]
         dma = pltpu.SemaphoreType.DMA
         return pl.pallas_call(
@@ -575,7 +576,7 @@
                 dma((9,)),
             ],
             compiler_params=pltpu.CompilerParams(
-                collective_id=0, has_side_effects=True, vmem_limit_bytes=67_043_328
+                collective_id=0, has_side_effects=True, vmem_limit_bytes=66_850_000
             ),
         )(
             frame_clip.reshape(1, -1), owner.reshape(1, -1), activations, conv_weight,

time: 31.1 us -> 30.9 us (level)
  no operation moved by 1% of the time
where the time goes in v4:
time: 30.9 us; the launch traced here: 30.8 us
  Pallas kernels  29.3 us (95%)
  local copies, waits for them, and re-layouts  1.47 us (5%)
    pallas_call x1, Pallas kernels, shards(): pl.pallas_call(functools.partial(kernel, (n_tm, n_space, capacity, chunks...  29.3 us
    unnamed x1, local copies, waits for them, and re-layouts  1.47 us

profile of v4, /device:TPU:0, one launch (start us, length us, event | category | flops | bytes accessed | tf_op | source)
XLA Modules:
  0.0 30.8 jit_solution(15742376710334411520)
XLA Ops:
  0.0 29.3 %shard_map.73 = bf16[1,16,16,128]{3,2,1,0:T(8,128)(2,1)} custom-call(s32[1,2]{1,0:T(1,128)} %bitcast.8, s32[1,8]{1,0:T(1,128)} %bitcast.9, bf16[64,2,8,256]{3,2,1,0:T(8,128)(2,1)} %act_in.1, bf16[3,3,3,128,128]{4,3,2,1,0:T(8,128)(2,1)} %weight_in.1, f32[1,128]{1,0:T(1,128)} %bitcast.10, f32[1,128]{1,0:T(1,128)} %bitcast.11, bf16[4,32,128]{2,1,0:T(8,128)(2,1)} %bitcast.7), custom_call_target="tpu_custom_call" | custom-call | tf_op jit(solution)/shard_map/pallas_call | solution.py:536
  29.3 1.5 %copy.9 = bf16[1,16,16,128]{3,2,1,0:T(8,128)(2,1)} copy(bf16[1,16,16,128]{3,2,1,0:T(8,128)(2,1)} %shard_map.73) | data formatting | bytes 131072
